TPU v7x, 32 devices: a whole 2x2x4 slice. The times are simulated.
32 devices in a mesh: group: 2 (over x), dev: 16 (over z, y, core).
Axes of the slice: x: 2, y: 2, z: 4, core: 2. Of those that a mesh axis runs over, the one named last changes fastest.
Arguments:
- positions: float32 [256, 3, 544], P(('group', 'dev')), may hold values from -6 to 6
- analysis: float32 [289, 544], replicated, may hold values from -0.25 to 0.25
- synthesis: float32 [544, 289], replicated, may hold values from -0.375 to 0.375
- stiffness: float32 [289], replicated, may hold values from 0.1 to 10
- owner: int32 [1088, 1], P(('group', 'dev')), may hold values from 0 to 15; in each aligned block of 34 rows (0 to 33, 34 to 67, ...) at most 4 rows name the same one
- ulist: int32 [2048, 4], P(('group', 'dev')), may hold values from 0 to 191, as said below
Outputs:
- moved: float32 [256, 3, 544], P(('group', 'dev'))
- velocity: float32 [256, 3, 544], P(('group', 'dev'))
Inputs may be any that keep to these rules, and one draw needn't show every extreme that they name: On the points of one device, no owner receives more than 4 blocks, and some owner receives exactly 4. `ulist`: entry 0 of row r is 64 + r % 64, the slot itself.
All inputs are finite; a program needn't handle non-finite values.
Results may differ from a plain program's by a relative error of at most 0.00011.
Values sent between devices are 32-bit elements; how exact they have to be, the bound alone decides.
A program may use at most 64 MiB of HBM per device.

v0:
```python
import math

import jax
import jax.numpy as jnp
from jax import lax
from jax.sharding import PartitionSpec as P

P_SIZE = 544
LEAF = 128
KNEAR = 4
C_DEV = 8
BLK_DEV = 34


SOFTENING = 0.25
KERNEL = 1.0 / (8.0 * math.pi)
TIME_STEP = 0.02
PRECISE = lax.Precision.HIGHEST


def with_halo(block, sides, width):
    for axis, dim in sides:
        count = lax.axis_size(axis)
        forward = [(i, i + 1) for i in range(count - 1)]
        backward = [(target, source) for source, target in forward]
        low = lax.ppermute(
            lax.slice_in_dim(block, block.shape[dim] - width, None, axis=dim), axis, forward
        )
        high = lax.ppermute(lax.slice_in_dim(block, 0, width, axis=dim), axis, backward)
        block = jnp.concatenate([low, block, high], axis=dim)
    return block


def stokeslet(targets, sources):
    offset = targets[:, :, :, None] - sources[:, 0:3, None, :]
    forces = sources[:, 3:6, None, :]
    dist_sq = jnp.sum(offset * offset, axis=1) + SOFTENING
    kernel_scale = KERNEL / (dist_sq * jnp.sqrt(dist_sq))
    projected = jnp.sum(offset * forces, axis=1)
    summed = ((dist_sq + SOFTENING) * kernel_scale)[:, None] * forces + (projected * kernel_scale)[
        :, None
    ] * offset
    return jnp.sum(summed, axis=3)


def to_blocks(values):
    return values.transpose(1, 0, 2).reshape(3, BLK_DEV, LEAF).transpose(1, 0, 2)


def from_blocks(values):
    return values.transpose(1, 0, 2).reshape(3, C_DEV, P_SIZE).transpose(1, 0, 2)


def filtered(shape_field, analysis, synthesis):
    coeffs = jnp.einsum("ckp,mp->ckm", shape_field, analysis, precision=PRECISE)
    return jnp.einsum("ckm,pm->ckp", coeffs, synthesis, precision=PRECISE)


def shards(positions, analysis, synthesis, stiffness, owner, ulist):
    dev_count = lax.axis_size("dev")
    capacity = (BLK_DEV + dev_count - 1) // dev_count + 1
    slot_count = capacity * dev_count
    owner_dev = owner[:, 0]
    same_owner = owner_dev[:, None] == owner_dev[None, :]
    order_idx = jnp.arange(BLK_DEV, dtype=jnp.int32)
    earlier = order_idx[None, :] < order_idx[:, None]
    block_rank = jnp.sum(jnp.where(same_owner & earlier, 1, 0), axis=1).astype(jnp.int32)
    send_slot = owner_dev * capacity + block_rank
    onehot = (send_slot[:, None] == jnp.arange(slot_count, dtype=jnp.int32)[None, :]).astype(
        jnp.float32
    )
    batch_size = math.gcd(slot_count, 16)
    shape_field = positions
    coeffs = jnp.einsum("ckp,mp->ckm", shape_field, analysis, precision=PRECISE)
    forces = -jnp.einsum("ckm,pm->ckp", coeffs * stiffness, synthesis, precision=PRECISE)
    payload = jnp.concatenate([to_blocks(shape_field), to_blocks(forces)], axis=1).reshape(
        BLK_DEV, 6 * LEAF
    )
    packed = jnp.dot(onehot.T, payload, precision=PRECISE).reshape(dev_count, capacity, 6 * LEAF)
    arrived = lax.all_to_all(packed, "dev", split_axis=0, concat_axis=0, tiled=True).reshape(
        slot_count, 6, LEAF
    )
    near_data = with_halo(arrived[None], (("group", 0),), 1)
    near_data = near_data.reshape(3 * slot_count, 6, LEAF)

    def per_batch(batch_pair):
        targets, lists = batch_pair
        summed = jnp.zeros((targets.shape[0], 3, LEAF), jnp.float32)
        for entry in range(KNEAR):
            summed = summed + stokeslet(targets, near_data[lists[:, entry]])
        return summed

    flows = lax.map(
        per_batch,
        (arrived[:, 0:3].reshape(-1, batch_size, 3, LEAF), ulist.reshape(-1, batch_size, KNEAR)),
    )
    flows = flows.reshape(dev_count, capacity, 3 * LEAF)
    returned = lax.all_to_all(flows, "dev", split_axis=0, concat_axis=0, tiled=True).reshape(
        slot_count, 3 * LEAF
    )
    velocity = from_blocks(jnp.dot(onehot, returned, precision=PRECISE).reshape(BLK_DEV, 3, LEAF))
    shape_field = filtered(shape_field + TIME_STEP * velocity, analysis, synthesis)
    return (shape_field, velocity)


def solution(mesh):
    placed = (
        P(("group", "dev"), None, None),
        P(),
        P(),
        P(),
        P(("group", "dev"), None),
        P(("group", "dev"), None),
    )
    return jax.shard_map(
        shards,
        mesh=mesh,
        in_specs=placed,
        out_specs=(P(("group", "dev"), None, None), P(("group", "dev"), None, None)),
        check_vma=False,
    )
```

profile of v0, /device:TPU:0, one launch (start us, length us, event | category | flops | bytes accessed | tf_op | source)
XLA Modules:
  0.0 133.2 jit_solution(3900462287750983616)
XLA Ops:
  0.7 1.9 %convolution_multiply_fusion = f32[8,3,289]{2,0,1:T(8,128)S(1)} fusion(f32[8,3,544]{2,0,1:T(8,128)} %param.8, f32[289,544]{1,0:T(8,128)} %param.9, f32[289]{0:T(512)} %param.11), kind=kOutput, calls=%fused_computation.66 | convolution fusion | flops 45285144 | bytes 709988 | tf_op jit(solution)/shard_map/ckp,mp->ckm/dot_general | solution.py:74
  4.1 16.2 %all_to_all.10 = f32[16,4,768]{2,1,0:T(4,128)S(1)} all-to-all(f32[16,4,768]{2,1,0:T(4,128)S(1)} %copy.22), channel_id=1, replica_groups=mesh['group'=2,'dev'=16] {'dev'}, dimensions={0} | all-to-all | bytes 393216 | tf_op jit(solution)/shard_map/all_to_all | solution.py:80
  20.4 3.4 %collective-permute-start = (f32[1,64,6,128]{3,2,1,0:T(8,128)S(1)}, f32[1,64,6,128]{3,2,1,0:T(8,128)S(1)}, u32[]{:S(2)}, u32[]{:S(2)}) collective-permute-start(f32[1,64,6,128]{3,2,1,0:T(8,128)S(1)} %broadcast_in_dim_reshape.3), channel_id=1, source_target_pairs={{0,16},{1,17},{2,18},{3,19},{4,20},{5,21},{6,22},{7,23},{8,24},{9,... | collective-permute-start | bytes 589832 | tf_op jit(solution)/shard_map/ppermute | solution.py:26
  25.3 3.9 %collective-permute-done = f32[1,64,6,128]{3,2,1,0:T(8,128)S(1)} collective-permute-done((f32[1,64,6,128]{3,2,1,0:T(8,128)S(1)}, f32[1,64,6,128]{3,2,1,0:T(8,128)S(1)}, u32[]{:S(2)}, u32[]{:S(2)}) %collective-permute-start) | collective-permute-done | bytes 196640 | tf_op jit(solution)/shard_map/ppermute | solution.py:26
  29.2 4.1 %collective-permute-done.1 = f32[1,64,6,128]{3,2,1,0:T(8,128)S(1)} collective-permute-done((f32[1,64,6,128]{3,2,1,0:T(8,128)S(1)}, f32[1,64,6,128]{3,2,1,0:T(8,128)S(1)}, u32[]{:S(2)}, u32[]{:S(2)}) %collective-permute-start.1) | collective-permute-done | bytes 196640 | tf_op jit(solution)/shard_map/ppermute | solution.py:29
  34.4 86.1 %while.13 = (s32[]{:T(128)}, f32[4,16,3,128]{3,2,1,0:T(4,128)S(1)}, f32[4,16,3,128]{3,2,1,0:T(4,128)S(1)}, s32[4,16,4]{1,0,2:T(4,128)S(1)}, f32[192,6,128]{2,1,0:T(8,128)}, /*index=5*/s32[]{:T(128)}) while((s32[]{:T(128)}, f32[4,16,3,128]{3,2,1,0:T(4,128)S(1)}, f32[4,16,3,128]{3,2,1,0:T(4,128)S(1)}, s32[4,16,4]{1,0,2:T(4,128)S(1)}, ...), condition=%wide.region_14.15_spmd, body=%wide.region_1.14_spmd.sunk | while | flops 35649728 | bytes 35161680 | solution.py:93
  34.4 1.7 %gather_fusion.3 = f32[16,6,128]{2,1,0:T(8,128)S(1)} fusion(f32[192,6,128]{2,1,0:T(8,128)} %get-tuple-element.270, s32[1024]{0:T(1024)S(1)} %get-tuple-element.231), kind=kCustom, calls=%fused_computation.clone.1 | custom fusion | bytes 98368 | tf_op jit(solution)/shard_map/while/body/eval_jaxpr/gather | solution.py:90
  37.8 1.7 %gather_fusion.1 = f32[16,6,128]{2,1,0:T(8,128)S(1)} fusion(f32[192,6,128]{2,1,0:T(8,128)} %get-tuple-element.270, s32[1024]{0:T(1024)S(1)} %get-tuple-element.225), kind=kCustom, calls=%fused_computation.1.clone.1 | custom fusion | bytes 98368 | tf_op jit(solution)/shard_map/while/body/eval_jaxpr/gather | solution.py:90
  39.6 1.7 %gather_fusion.2 = f32[16,6,128]{2,1,0:T(8,128)S(1)} fusion(f32[192,6,128]{2,1,0:T(8,128)} %get-tuple-element.270, s32[1024]{0:T(1024)S(1)} %get-tuple-element.228), kind=kCustom, calls=%fused_computation.3.clone.1 | custom fusion | bytes 98368 | tf_op jit(solution)/shard_map/while/body/eval_jaxpr/gather | solution.py:90
  41.3 3.3 %fusion.74 = (f32[16,128,128]{2,1,0:T(8,128)S(1)}, f32[16,128,128]{2,1,0:T(8,128)S(1)}, f32[16,128,128]{2,1,0:T(8,128)S(1)}, f32[16,128,128]{2,1,0:T(8,128)S(1)}, f32[16,3,128]{2,1,0:T(4,128)S(1)}) fusion(f32[16,3,128]{2,1,0:T(4,128)S(1)} %get-tuple-element.226, f32[16,3,128]{2,1,0:T(4,128)S(1)} %dynamic-slice_bitcast_fusion.2, ...), kind=kLoop, calls=%fused_computation.20.clone.1 | loop fusion | flops 10741760 | bytes 6488064 | tf_op jit(solution)/shard_map/while/body/eval_jaxpr/reduce_sum | solution.py:37
  45.1 1.8 %add_multiply_fusion.9 = (f32[16,128,128]{2,1,0:T(8,128)}, f32[16,128,128]{2,1,0:T(8,128)}) fusion(f32[16,128,128]{2,1,0:T(8,128)S(1)} %get-tuple-element.238, f32[16,128,128]{2,1,0:T(8,128)S(1)} %get-tuple-element.239), kind=kLoop, calls=%fused_computation.42.clone.1 | loop fusion | flops 1572864 | bytes 4194304 | tf_op jit(solution)/shard_map/while/body/eval_jaxpr/mul | solution.py:40
  48.7 3.6 %fusion.75 = (f32[16,128,128]{2,1,0:T(8,128)S(1)}, f32[16,128,128]{2,1,0:T(8,128)S(1)}, f32[16,3,128]{2,1,0:T(4,128)S(1)}) fusion(f32[16,3,128]{2,1,0:T(4,128)S(1)} %get-tuple-element.221, f32[16,3,128]{2,1,0:T(4,128)S(1)} %dynamic-slice_bitcast_fusion.2, f32[16,3,128]{2,1,0:T(4,128)S(1)} %get-tuple-element.222, ...), kind=kLoop, calls=%fused_computation.24.clone.1 | loop fusion | flops 7333888 | bytes 4341760 | tf_op jit(solution)/shard_map/while/body/eval_jaxpr/reduce_sum | solution.py:37
  52.7 3.1 %fusion.76 = (f32[16,3,128]{2,1,0:T(4,128)S(1)}, f32[16,3,128]{2,1,0:T(4,128)S(1)}) fusion(f32[16,128,128]{2,1,0:T(8,128)S(1)} %get-tuple-element.244, f32[16,3,128]{2,1,0:T(4,128)S(1)} %get-tuple-element.222, f32[16,128,128]{2,1,0:T(8,128)S(1)} %get-tuple-element.245, f32[16,3,128]{2,1,0:T(4,128)S(1)} %get-tuple-element.221, ...), kind=kLoop, calls=%fused_computation.27.clone.1 | loop fusion | flops 7852032 | bytes 4366336 | tf_op jit(solution)/shard_map/while/body/eval_jaxpr/reduce_sum | solution.py:43
  55.9 1.7 %gather_fusion.3 = f32[16,6,128]{2,1,0:T(8,128)S(1)} fusion(f32[192,6,128]{2,1,0:T(8,128)} %get-tuple-element.270, s32[1024]{0:T(1024)S(1)} %get-tuple-element.231), kind=kCustom, calls=%fused_computation.clone.1 | custom fusion | bytes 98368 | tf_op jit(solution)/shard_map/while/body/eval_jaxpr/gather | solution.py:90
  59.4 1.7 %gather_fusion.1 = f32[16,6,128]{2,1,0:T(8,128)S(1)} fusion(f32[192,6,128]{2,1,0:T(8,128)} %get-tuple-element.270, s32[1024]{0:T(1024)S(1)} %get-tuple-element.225), kind=kCustom, calls=%fused_computation.1.clone.1 | custom fusion | bytes 98368 | tf_op jit(solution)/shard_map/while/body/eval_jaxpr/gather | solution.py:90
  61.1 1.7 %gather_fusion.2 = f32[16,6,128]{2,1,0:T(8,128)S(1)} fusion(f32[192,6,128]{2,1,0:T(8,128)} %get-tuple-element.270, s32[1024]{0:T(1024)S(1)} %get-tuple-element.228), kind=kCustom, calls=%fused_computation.3.clone.1 | custom fusion | bytes 98368 | tf_op jit(solution)/shard_map/while/body/eval_jaxpr/gather | solution.py:90
  62.8 3.3 %fusion.74 = (f32[16,128,128]{2,1,0:T(8,128)S(1)}, f32[16,128,128]{2,1,0:T(8,128)S(1)}, f32[16,128,128]{2,1,0:T(8,128)S(1)}, f32[16,128,128]{2,1,0:T(8,128)S(1)}, f32[16,3,128]{2,1,0:T(4,128)S(1)}) fusion(f32[16,3,128]{2,1,0:T(4,128)S(1)} %get-tuple-element.226, f32[16,3,128]{2,1,0:T(4,128)S(1)} %dynamic-slice_bitcast_fusion.2, ...), kind=kLoop, calls=%fused_computation.20.clone.1 | loop fusion | flops 10741760 | bytes 6488064 | tf_op jit(solution)/shard_map/while/body/eval_jaxpr/reduce_sum | solution.py:37
  66.7 1.8 %add_multiply_fusion.9 = (f32[16,128,128]{2,1,0:T(8,128)}, f32[16,128,128]{2,1,0:T(8,128)}) fusion(f32[16,128,128]{2,1,0:T(8,128)S(1)} %get-tuple-element.238, f32[16,128,128]{2,1,0:T(8,128)S(1)} %get-tuple-element.239), kind=kLoop, calls=%fused_computation.42.clone.1 | loop fusion | flops 1572864 | bytes 4194304 | tf_op jit(solution)/shard_map/while/body/eval_jaxpr/mul | solution.py:40
  70.2 3.6 %fusion.75 = (f32[16,128,128]{2,1,0:T(8,128)S(1)}, f32[16,128,128]{2,1,0:T(8,128)S(1)}, f32[16,3,128]{2,1,0:T(4,128)S(1)}) fusion(f32[16,3,128]{2,1,0:T(4,128)S(1)} %get-tuple-element.221, f32[16,3,128]{2,1,0:T(4,128)S(1)} %dynamic-slice_bitcast_fusion.2, f32[16,3,128]{2,1,0:T(4,128)S(1)} %get-tuple-element.222, ...), kind=kLoop, calls=%fused_computation.24.clone.1 | loop fusion | flops 7333888 | bytes 4341760 | tf_op jit(solution)/shard_map/while/body/eval_jaxpr/reduce_sum | solution.py:37
  74.3 3.1 %fusion.76 = (f32[16,3,128]{2,1,0:T(4,128)S(1)}, f32[16,3,128]{2,1,0:T(4,128)S(1)}) fusion(f32[16,128,128]{2,1,0:T(8,128)S(1)} %get-tuple-element.244, f32[16,3,128]{2,1,0:T(4,128)S(1)} %get-tuple-element.222, f32[16,128,128]{2,1,0:T(8,128)S(1)} %get-tuple-element.245, f32[16,3,128]{2,1,0:T(4,128)S(1)} %get-tuple-element.221, ...), kind=kLoop, calls=%fused_computation.27.clone.1 | loop fusion | flops 7852032 | bytes 4366336 | tf_op jit(solution)/shard_map/while/body/eval_jaxpr/reduce_sum | solution.py:43
  77.5 1.7 %gather_fusion.3 = f32[16,6,128]{2,1,0:T(8,128)S(1)} fusion(f32[192,6,128]{2,1,0:T(8,128)} %get-tuple-element.270, s32[1024]{0:T(1024)S(1)} %get-tuple-element.231), kind=kCustom, calls=%fused_computation.clone.1 | custom fusion | bytes 98368 | tf_op jit(solution)/shard_map/while/body/eval_jaxpr/gather | solution.py:90
  80.9 1.7 %gather_fusion.1 = f32[16,6,128]{2,1,0:T(8,128)S(1)} fusion(f32[192,6,128]{2,1,0:T(8,128)} %get-tuple-element.270, s32[1024]{0:T(1024)S(1)} %get-tuple-element.225), kind=kCustom, calls=%fused_computation.1.clone.1 | custom fusion | bytes 98368 | tf_op jit(solution)/shard_map/while/body/eval_jaxpr/gather | solution.py:90
  84.4 3.3 %fusion.74 = (f32[16,128,128]{2,1,0:T(8,128)S(1)}, f32[16,128,128]{2,1,0:T(8,128)S(1)}, f32[16,128,128]{2,1,0:T(8,128)S(1)}, f32[16,128,128]{2,1,0:T(8,128)S(1)}, f32[16,3,128]{2,1,0:T(4,128)S(1)}) fusion(f32[16,3,128]{2,1,0:T(4,128)S(1)} %get-tuple-element.226, f32[16,3,128]{2,1,0:T(4,128)S(1)} %dynamic-slice_bitcast_fusion.2, ...), kind=kLoop, calls=%fused_computation.20.clone.1 | loop fusion | flops 10741760 | bytes 6488064 | tf_op jit(solution)/shard_map/while/body/eval_jaxpr/reduce_sum | solution.py:37
  88.2 1.8 %add_multiply_fusion.9 = (f32[16,128,128]{2,1,0:T(8,128)}, f32[16,128,128]{2,1,0:T(8,128)}) fusion(f32[16,128,128]{2,1,0:T(8,128)S(1)} %get-tuple-element.238, f32[16,128,128]{2,1,0:T(8,128)S(1)} %get-tuple-element.239), kind=kLoop, calls=%fused_computation.42.clone.1 | loop fusion | flops 1572864 | bytes 4194304 | tf_op jit(solution)/shard_map/while/body/eval_jaxpr/mul | solution.py:40
  91.8 3.6 %fusion.75 = (f32[16,128,128]{2,1,0:T(8,128)S(1)}, f32[16,128,128]{2,1,0:T(8,128)S(1)}, f32[16,3,128]{2,1,0:T(4,128)S(1)}) fusion(f32[16,3,128]{2,1,0:T(4,128)S(1)} %get-tuple-element.221, f32[16,3,128]{2,1,0:T(4,128)S(1)} %dynamic-slice_bitcast_fusion.2, f32[16,3,128]{2,1,0:T(4,128)S(1)} %get-tuple-element.222, ...), kind=kLoop, calls=%fused_computation.24.clone.1 | loop fusion | flops 7333888 | bytes 4341760 | tf_op jit(solution)/shard_map/while/body/eval_jaxpr/reduce_sum | solution.py:37
  95.8 3.1 %fusion.76 = (f32[16,3,128]{2,1,0:T(4,128)S(1)}, f32[16,3,128]{2,1,0:T(4,128)S(1)}) fusion(f32[16,128,128]{2,1,0:T(8,128)S(1)} %get-tuple-element.244, f32[16,3,128]{2,1,0:T(4,128)S(1)} %get-tuple-element.222, f32[16,128,128]{2,1,0:T(8,128)S(1)} %get-tuple-element.245, f32[16,3,128]{2,1,0:T(4,128)S(1)} %get-tuple-element.221, ...), kind=kLoop, calls=%fused_computation.27.clone.1 | loop fusion | flops 7852032 | bytes 4366336 | tf_op jit(solution)/shard_map/while/body/eval_jaxpr/reduce_sum | solution.py:43
  102.4 1.7 %gather_fusion.1 = f32[16,6,128]{2,1,0:T(8,128)S(1)} fusion(f32[192,6,128]{2,1,0:T(8,128)} %get-tuple-element.270, s32[1024]{0:T(1024)S(1)} %get-tuple-element.225), kind=kCustom, calls=%fused_computation.1.clone.1 | custom fusion | bytes 98368 | tf_op jit(solution)/shard_map/while/body/eval_jaxpr/gather | solution.py:90
  105.9 3.3 %fusion.74 = (f32[16,128,128]{2,1,0:T(8,128)S(1)}, f32[16,128,128]{2,1,0:T(8,128)S(1)}, f32[16,128,128]{2,1,0:T(8,128)S(1)}, f32[16,128,128]{2,1,0:T(8,128)S(1)}, f32[16,3,128]{2,1,0:T(4,128)S(1)}) fusion(f32[16,3,128]{2,1,0:T(4,128)S(1)} %get-tuple-element.226, f32[16,3,128]{2,1,0:T(4,128)S(1)} %dynamic-slice_bitcast_fusion.2, ...), kind=kLoop, calls=%fused_computation.20.clone.1 | loop fusion | flops 10741760 | bytes 6488064 | tf_op jit(solution)/shard_map/while/body/eval_jaxpr/reduce_sum | solution.py:37
  109.7 1.8 %add_multiply_fusion.9 = (f32[16,128,128]{2,1,0:T(8,128)}, f32[16,128,128]{2,1,0:T(8,128)}) fusion(f32[16,128,128]{2,1,0:T(8,128)S(1)} %get-tuple-element.238, f32[16,128,128]{2,1,0:T(8,128)S(1)} %get-tuple-element.239), kind=kLoop, calls=%fused_computation.42.clone.1 | loop fusion | flops 1572864 | bytes 4194304 | tf_op jit(solution)/shard_map/while/body/eval_jaxpr/mul | solution.py:40
  113.3 3.6 %fusion.75 = (f32[16,128,128]{2,1,0:T(8,128)S(1)}, f32[16,128,128]{2,1,0:T(8,128)S(1)}, f32[16,3,128]{2,1,0:T(4,128)S(1)}) fusion(f32[16,3,128]{2,1,0:T(4,128)S(1)} %get-tuple-element.221, f32[16,3,128]{2,1,0:T(4,128)S(1)} %dynamic-slice_bitcast_fusion.2, f32[16,3,128]{2,1,0:T(4,128)S(1)} %get-tuple-element.222, ...), kind=kLoop, calls=%fused_computation.24.clone.1 | loop fusion | flops 7333888 | bytes 4341760 | tf_op jit(solution)/shard_map/while/body/eval_jaxpr/reduce_sum | solution.py:37
  117.3 3.1 %fusion.76 = (f32[16,3,128]{2,1,0:T(4,128)S(1)}, f32[16,3,128]{2,1,0:T(4,128)S(1)}) fusion(f32[16,128,128]{2,1,0:T(8,128)S(1)} %get-tuple-element.244, f32[16,3,128]{2,1,0:T(4,128)S(1)} %get-tuple-element.222, f32[16,128,128]{2,1,0:T(8,128)S(1)} %get-tuple-element.245, f32[16,3,128]{2,1,0:T(4,128)S(1)} %get-tuple-element.221, ...), kind=kLoop, calls=%fused_computation.27.clone.1 | loop fusion | flops 7852032 | bytes 4366336 | tf_op jit(solution)/shard_map/while/body/eval_jaxpr/reduce_sum | solution.py:43
  120.6 10.4 %all_to_all.11 = f32[16,4,384]{2,1,0:T(4,128)S(1)} all-to-all(f32[16,4,384]{2,1,0:T(4,128)S(1)} %reshape.183), channel_id=1, replica_groups=mesh['group'=2,'dev'=16] {'dev'}, dimensions={0} | all-to-all | bytes 196608 | tf_op jit(solution)/shard_map/all_to_all | solution.py:98
  (99 shorter events, 29.3 us)
Async XLA Ops:
  0.6 2.0 %copy-start = (f32[544,289]{0,1:T(8,128)S(1)}, f32[544,289]{0,1:T(8,128)}, u32[]{:S(2)}) copy-start(f32[544,289]{0,1:T(8,128)} %param.10) | copy-start | bytes 1886596
  0.6 2.6 %copy-start.2 = (f32[8,3,544]{2,0,1:T(8,128)S(1)}, f32[8,3,544]{2,0,1:T(8,128)}, u32[]{:S(2)}) copy-start(f32[8,3,544]{2,0,1:T(8,128)} %param.8) | copy-start | bytes 156676
  2.6 0.9 copy-start.5
  3.4 21.7 %copy-start.4 = (s32[64,4]{0,1:T(4,128)S(1)}, s32[64,4]{0,1:T(4,128)}, u32[]{:S(2)}) copy-start(s32[64,4]{0,1:T(4,128)} %param.13) | copy-start | bytes 3076
  20.4 8.9 %collective-permute-start = (f32[1,64,6,128]{3,2,1,0:T(8,128)S(1)}, f32[1,64,6,128]{3,2,1,0:T(8,128)S(1)}, u32[]{:S(2)}, u32[]{:S(2)}) collective-permute-start(f32[1,64,6,128]{3,2,1,0:T(8,128)S(1)} %broadcast_in_dim_reshape.3), channel_id=1, source_target_pairs={{0,16},{1,17},{2,18},{3,19},{4,20},{5,21},{6,22},{7,23},{8,24},{9,... | collective-permute-start | bytes 589832 | tf_op jit(solution)/shard_map/ppermute | solution.py:26
  23.8 9.6 %collective-permute-start.1 = (f32[1,64,6,128]{3,2,1,0:T(8,128)S(1)}, f32[1,64,6,128]{3,2,1,0:T(8,128)S(1)}, u32[]{:S(2)}, u32[]{:S(2)}) collective-permute-start(f32[1,64,6,128]{3,2,1,0:T(8,128)S(1)} %broadcast_in_dim_reshape.3), channel_id=1, source_target_pairs={{16,0},{17,1},{18,2},{19,3},{20,4},{21,5},{22,6},{23,7},{24,8},{25... | collective-permute-start | bytes 589832 | tf_op jit(solution)/shard_map/ppermute | solution.py:29
  120.5 10.9 %copy-start.1 = (f32[289,544]{1,0:T(8,128)S(1)}, f32[289,544]{1,0:T(8,128)}, u32[]{:S(2)}) copy-start(f32[289,544]{1,0:T(8,128)} %param.9) | copy-start | bytes 1886596
  131.3 1.9 %copy-start.3 = (f32[3,8,544]{2,1,0:T(8,128)}, f32[3,8,544]{2,1,0:T(8,128)S(1)}, u32[]{:S(2)}) copy-start(f32[3,8,544]{2,1,0:T(8,128)S(1)} %reshape.185) | copy-start | bytes 156676
where the time goes:
time: 134 us; the launch traced here: 133 us
  other arithmetic  59.3 us (44%)
  local copies, waits for them, and re-layouts  28.2 us (21%)
  blocking collectives  26.6 us (20%)
  waiting for transfers between devices  8.04 us (6%)
  matrix products  4.87 us (4%)
  starting transfers between devices  4.7 us (4%)
    reduce_sum x12, other arithmetic, stokeslet(): dist_sq = jnp.sum(offset * offset, axis=1) + SOFTENING  32.5 us
    gather x16, local copies, waits for them, and re-layouts, per_batch(): summed = summed + stokeslet(targets, near_data[lists[:, entry]])  27 us
    all_to_all x1, blocking collectives, shards(): lax.all_to_all(packed, 'dev', split_axis=0, concat_axis=0, tiled=True)  16.2 us
    mul x16, other arithmetic, stokeslet(): (dist_sq + SOFTENING) * kernel_scale  13.2 us
    reduce_sum x4, other arithmetic, stokeslet(): return jnp.sum(summed, axis=3)  12.3 us
    all_to_all x1, blocking collectives, shards(): lax.all_to_all(flows, 'dev', split_axis=0, concat_axis=0, tiled=True)  10.4 us
    ppermute x1, waiting for transfers between devices, with_halo(): lax.ppermute(lax.slice_in_dim(block, 0, width, axis=dim), axis, backward)  4.13 us
    ppermute x1, waiting for transfers between devices, with_halo(): lax.ppermute(lax.slice_in_dim(block, block.shape[dim] - width, None, axis...  3.91 us
  transfers between devices with their start and end apart: 2, of which 2 were waited for; matrix products, arithmetic and copies ran while one was open for 0% of the time, Pallas kernels for 0%

commit v1 on v0

--- a/solution.py
+++ b/solution.py
@@ -3,6 +3,8 @@
 import jax
 import jax.numpy as jnp
 from jax import lax
+from jax.experimental import pallas as pl
+from jax.experimental.pallas import tpu as pltpu
 from jax.sharding import PartitionSpec as P
 
 P_SIZE = 544
@@ -31,16 +33,91 @@
     return block
 
 
-def stokeslet(targets, sources):
-    offset = targets[:, :, :, None] - sources[:, 0:3, None, :]
-    forces = sources[:, 3:6, None, :]
-    dist_sq = jnp.sum(offset * offset, axis=1) + SOFTENING
-    kernel_scale = KERNEL / (dist_sq * jnp.sqrt(dist_sq))
-    projected = jnp.sum(offset * forces, axis=1)
-    summed = ((dist_sq + SOFTENING) * kernel_scale)[:, None] * forces + (projected * kernel_scale)[
-        :, None
-    ] * offset
-    return jnp.sum(summed, axis=3)
+def split3(value):
+    first = value.astype(jnp.bfloat16)
+    rest = value - first.astype(jnp.float32)
+    second = rest.astype(jnp.bfloat16)
+    third = (rest - second.astype(jnp.float32)).astype(jnp.bfloat16)
+    return first, second, third
+
+
+def split2(value):
+    first = value.astype(jnp.bfloat16)
+    return first, (value - first.astype(jnp.float32)).astype(jnp.bfloat16)
+
+
+def near_kernel(lists_ref, near_ref, flows_ref, table_ref):
+    total = near_ref.shape[0]
+    slot_count = flows_ref.shape[0]
+    zeros4 = jnp.zeros((4, LEAF), jnp.float32)
+    ones = jnp.ones((1, LEAF), jnp.float32)
+
+    def prepare(slot, carry):
+        data = near_ref[slot]
+        y, f = data[0:3], data[3:6]
+        y_sq = jnp.sum(y * y, axis=0, keepdims=True) + SOFTENING
+        yf = -jnp.sum(y * f, axis=0, keepdims=True)
+        dist = jnp.concatenate([-2.0 * y, y_sq, ones, jnp.zeros((3, LEAF), jnp.float32)], axis=0)
+        proj = jnp.concatenate([f, yf, zeros4], axis=0)
+        d1, d2, d3 = [piece.astype(jnp.float32) for piece in split3(dist)]
+        p1, p2, p3 = [piece.astype(jnp.float32) for piece in split3(proj)]
+        w_f = jnp.concatenate([f * KERNEL, jnp.zeros((5, LEAF), jnp.float32)], axis=0)
+        w_y = jnp.concatenate([-KERNEL * y, KERNEL * ones, zeros4], axis=0)
+        f1, f2 = [piece.astype(jnp.float32) for piece in split2(w_f)]
+        y1, y2 = [piece.astype(jnp.float32) for piece in split2(w_y)]
+        left = jnp.concatenate([d1, d2, d3, d1, d2, d1, f1, f2], axis=0)
+        right = jnp.concatenate([p1, p2, p3, p1, p2, p1, y1, y2], axis=0)
+        table_ref[slot, :, 0:LEAF] = left.astype(jnp.bfloat16)
+        table_ref[slot, :, LEAF:] = right.astype(jnp.bfloat16)
+        return carry
+
+    lax.fori_loop(0, total, prepare, 0, unroll=4)
+    own = slot_count
+
+    def one_slot(slot, carry):
+        x = near_ref[own + slot][0:3]
+        x_sq = jnp.sum(x * x, axis=0, keepdims=True)
+        base = jnp.concatenate([x, ones, x_sq, jnp.zeros((3, LEAF), jnp.float32)], axis=0)
+        t1, t2, t3 = [piece.astype(jnp.float32) for piece in split3(base)]
+        target = jnp.concatenate([t1, t1, t1, t2, t2, t3], axis=0).T.astype(jnp.bfloat16)
+        total_c = None
+        for entry in range(KNEAR):
+            source = lists_ref[slot * KNEAR + entry]
+            rows = table_ref[source]
+            both = jnp.dot(target, rows[0:48], preferred_element_type=jnp.float32)
+            rr, projected = both[:, 0:LEAF], both[:, LEAF:]
+            inv = lax.rsqrt(rr)
+            inv3 = inv * inv * inv
+            a1, a2 = split2(inv + SOFTENING * inv3)
+            b1, b2 = split2(projected * inv3)
+            w_f, w_y = rows[48:64, 0:LEAF], rows[48:64, LEAF:]
+            values = jnp.concatenate([a1, a2, b1, b2], axis=1)
+            weights = jnp.concatenate([w_f, w_f, w_y, w_y], axis=1)
+            part = lax.dot_general(
+                values, weights, (((1,), (1,)), ((), ())), preferred_element_type=jnp.float32
+            )
+            total_c = part if total_c is None else total_c + part
+        turned = total_c.T
+        turned = turned[0:8] + turned[8:16]
+        flows_ref[slot] = turned[0:3] + x * turned[3:4]
+        return carry
+
+    lax.fori_loop(0, slot_count, one_slot, 0, unroll=2)
+
+
+def near_sum(near_data, lists):
+    total = near_data.shape[0]
+    slot_count = lists.shape[0]
+    return pl.pallas_call(
+        near_kernel,
+        out_shape=jax.ShapeDtypeStruct((slot_count, 3, LEAF), jnp.float32),
+        in_specs=[
+            pl.BlockSpec(memory_space=pltpu.SMEM),
+            pl.BlockSpec(memory_space=pltpu.VMEM),
+        ],
+        out_specs=pl.BlockSpec(memory_space=pltpu.VMEM),
+        scratch_shapes=[pltpu.VMEM((total, 64, 2 * LEAF), jnp.bfloat16)],
+    )(lists.reshape(-1), near_data)
 
 
 def to_blocks(values):
@@ -69,7 +146,6 @@
     onehot = (send_slot[:, None] == jnp.arange(slot_count, dtype=jnp.int32)[None, :]).astype(
         jnp.float32
     )
-    batch_size = math.gcd(slot_count, 16)
     shape_field = positions
     coeffs = jnp.einsum("ckp,mp->ckm", shape_field, analysis, precision=PRECISE)
     forces = -jnp.einsum("ckm,pm->ckp", coeffs * stiffness, synthesis, precision=PRECISE)
@@ -83,17 +159,7 @@
     near_data = with_halo(arrived[None], (("group", 0),), 1)
     near_data = near_data.reshape(3 * slot_count, 6, LEAF)
 
-    def per_batch(batch_pair):
-        targets, lists = batch_pair
-        summed = jnp.zeros((targets.shape[0], 3, LEAF), jnp.float32)
-        for entry in range(KNEAR):
-            summed = summed + stokeslet(targets, near_data[lists[:, entry]])
-        return summed
-
-    flows = lax.map(
-        per_batch,
-        (arrived[:, 0:3].reshape(-1, batch_size, 3, LEAF), ulist.reshape(-1, batch_size, KNEAR)),
-    )
+    flows = near_sum(near_data, ulist)
     flows = flows.reshape(dev_count, capacity, 3 * LEAF)
     returned = lax.all_to_all(flows, "dev", split_axis=0, concat_axis=0, tiled=True).reshape(
         slot_count, 3 * LEAF

time: 134 us -> 85.5 us (0.64)
  other arithmetic: 59.3 us -> 1.18 us
  Pallas kernels: 0 us -> 35.2 us
  local copies, waits for them, and re-layouts: 28.2 us -> 4.46 us
    reduce_sum x16 -> x0, other arithmetic: 44.7 us -> none  [the longest x12 32.5 us: stokeslet(): dist_sq = jnp.sum(offset * offset, axis=1) + SOFTENING]
    pallas_call x0 -> x1, Pallas kernels: none -> 35.2 us  [near_sum(): pl.pallas_call(near_kernel, out_shape=jax.ShapeDtypeStruct((slot_count, 3...]
    gather x16 -> x0, local copies, waits for them, and re-layouts: 27 us -> none  [per_batch(): summed = summed + stokeslet(targets, near_data[lists[:, entry]])]
    mul x16 -> x0, other arithmetic: 13.2 us -> none  [stokeslet(): (dist_sq + SOFTENING) * kernel_scale]
    unnamed x12 -> x15, local copies, waits for them, and re-layouts: 0.04 us -> 2.23 us
  transfers between devices with their start and end apart: 2 -> 2, of which waited for: 2 -> 2; matrix products, arithmetic and copies ran while one was open for 0% -> 1% of each run, Pallas kernels for 0% -> 0%
where the time goes in v1:
time: 85.5 us; the launch traced here: 85.1 us
  Pallas kernels  35.2 us (41%)
  blocking collectives  26.4 us (31%)
  waiting for transfers between devices  7.48 us (9%)
  matrix products  4.83 us (6%)
  starting transfers between devices  4.7 us (5%)
  local copies, waits for them, and re-layouts  4.46 us (5%)
  other arithmetic  1.18 us (1%)
    pallas_call x1, Pallas kernels, near_sum(): pl.pallas_call(near_kernel, out_shape=jax.ShapeDtypeStruct((slot_count, 3...  35.2 us
    all_to_all x1, blocking collectives, shards(): lax.all_to_all(packed, 'dev', split_axis=0, concat_axis=0, tiled=True)  16.2 us
    all_to_all x1, blocking collectives, shards(): lax.all_to_all(flows, 'dev', split_axis=0, concat_axis=0, tiled=True)  10.2 us
    ppermute x1, waiting for transfers between devices, with_halo(): lax.ppermute(lax.slice_in_dim(block, 0, width, axis=dim), axis, backward)  4.13 us
    ppermute x1, starting transfers between devices, with_halo(): lax.ppermute(lax.slice_in_dim(block, block.shape[dim] - width, None, axis...  3.41 us
    ppermute x1, waiting for transfers between devices, with_halo(): lax.ppermute(lax.slice_in_dim(block, block.shape[dim] - width, None, axis...  3.35 us
    unnamed x15, local copies, waits for them, and re-layouts  2.23 us
    dot_general x1, matrix products, shards(): coeffs = jnp.einsum('ckp,mp->ckm', shape_field, analysis, precision=PRECISE)  1.91 us
  transfers between devices with their start and end apart: 2, of which 2 were waited for; matrix products, arithmetic and copies ran while one was open for 1% of the time, Pallas kernels for 0%

profile of v1, /device:TPU:0, one launch (start us, length us, event | category | flops | bytes accessed | tf_op | source)
XLA Modules:
  0.0 85.1 jit_solution(15913536446969117489)
XLA Ops:
  0.6 0.0 copy-start
  0.7 0.7 copy-done.4
  1.4 1.9 %convolution_multiply_fusion = f32[8,3,289]{2,0,1:T(8,128)S(1)} fusion(f32[8,3,544]{2,0,1:T(8,128)} %param.6, f32[289,544]{1,0:T(8,128)} %param.7, f32[289]{0:T(512)S(1)} %copy-done.4), kind=kOutput, calls=%fused_computation.3 | convolution fusion | flops 45285144 | bytes 709988 | tf_op jit(solution)/shard_map/ckp,mp->ckm/dot_general | solution.py:150
  3.3 0.0 copy-done
  3.3 0.5 fusion
  3.9 0.0 copy-start.2
  3.9 0.1 reshape.54
  4.0 0.7 copy-done.2
  4.7 0.1 reshape.53
  4.9 0.0 copy-start.6
  4.9 0.6 copy-done.6
  5.6 0.2 select_reduce_fusion
  5.7 0.3 fusion.11
  6.0 0.1 copy.22
  6.2 16.2 %all_to_all.10 = f32[16,4,768]{2,1,0:T(4,128)S(1)} all-to-all(f32[16,4,768]{2,1,0:T(4,128)S(1)} %copy.22), channel_id=1, replica_groups=mesh['group'=2,'dev'=16] {'dev'}, dimensions={0} | all-to-all | bytes 393216 | tf_op jit(solution)/shard_map/all_to_all | solution.py:156
  22.4 0.1 broadcast_in_dim_reshape.3
  22.4 3.4 %collective-permute-start = (f32[1,64,6,128]{3,2,1,0:T(8,128)S(1)}, f32[1,64,6,128]{3,2,1,0:T(8,128)S(1)}, u32[]{:S(2)}, u32[]{:S(2)}) collective-permute-start(f32[1,64,6,128]{3,2,1,0:T(8,128)S(1)} %broadcast_in_dim_reshape.3), channel_id=1, source_target_pairs={{0,16},{1,17},{2,18},{3,19},{4,20},{5,21},{6,22},{7,23},{8,24},{9,... | collective-permute-start | bytes 589832 | tf_op jit(solution)/shard_map/ppermute | solution.py:28
  25.9 1.3 %collective-permute-start.1 = (f32[1,64,6,128]{3,2,1,0:T(8,128)S(1)}, f32[1,64,6,128]{3,2,1,0:T(8,128)S(1)}, u32[]{:S(2)}, u32[]{:S(2)}) collective-permute-start(f32[1,64,6,128]{3,2,1,0:T(8,128)S(1)} %broadcast_in_dim_reshape.3), channel_id=1, source_target_pairs={{16,0},{17,1},{18,2},{19,3},{20,4},{21,5},{22,6},{23,7},{24,8},{25... | collective-permute-start | bytes 589832 | tf_op jit(solution)/shard_map/ppermute | solution.py:31
  27.2 0.1 copy.19
  27.3 0.7 reshape.52.lists_ref
  27.9 3.4 %collective-permute-done = f32[1,64,6,128]{3,2,1,0:T(8,128)S(1)} collective-permute-done((f32[1,64,6,128]{3,2,1,0:T(8,128)S(1)}, f32[1,64,6,128]{3,2,1,0:T(8,128)S(1)}, u32[]{:S(2)}, u32[]{:S(2)}) %collective-permute-start) | collective-permute-done | bytes 196640 | tf_op jit(solution)/shard_map/ppermute | solution.py:28
  31.3 4.1 %collective-permute-done.1 = f32[1,64,6,128]{3,2,1,0:T(8,128)S(1)} collective-permute-done((f32[1,64,6,128]{3,2,1,0:T(8,128)S(1)}, f32[1,64,6,128]{3,2,1,0:T(8,128)S(1)}, u32[]{:S(2)}, u32[]{:S(2)}) %collective-permute-start.1) | collective-permute-done | bytes 196640 | tf_op jit(solution)/shard_map/ppermute | solution.py:31
  35.4 1.0 %pad_maximum_fusion = f32[3,64,6,128]{3,2,1,0:T(8,128)} fusion(f32[1,64,6,128]{3,2,1,0:T(8,128)S(1)} %collective-permute-done.1, f32[1,64,6,128]{3,2,1,0:T(8,128)S(1)} %broadcast_in_dim_reshape.3, f32[1,64,6,128]{3,2,1,0:T(8,128)S(1)} %collective-permute-done), kind=kLoop, calls=%fused_computation.4 | loop fusion | flops 294912 | bytes 1179648 | tf_op jit(solution)/shard_map/concatenate | solution.py:32
  36.4 35.2 %shard_map.77 = f32[64,3,128]{2,1,0:T(4,128)} custom-call(s32[256]{0:T(256)} %reshape.52.lists_ref, f32[192,6,128]{2,1,0:T(8,128)} %bitcast.43), custom_call_target="tpu_custom_call" | custom-call | tf_op jit(solution)/shard_map/pallas_call | solution.py:111
  71.6 1.0 %reshape.57 = f32[16,4,384]{2,1,0:T(4,128)S(1)} reshape(f32[64,3,128]{2,1,0:T(4,128)} %shard_map.77) | data formatting | bytes 196608 | tf_op jit(solution)/shard_map/reshape | solution.py:163
  72.6 10.2 %all_to_all.11 = f32[16,4,384]{2,1,0:T(4,128)S(1)} all-to-all(f32[16,4,384]{2,1,0:T(4,128)S(1)} %reshape.57), channel_id=1, replica_groups=mesh['group'=2,'dev'=16] {'dev'}, dimensions={0} | all-to-all | bytes 196608 | tf_op jit(solution)/shard_map/all_to_all | solution.py:164
  82.8 0.2 convolution_bitcast_fusion
  83.1 0.1 reshape.59
  83.2 0.0 copy-start.3
  83.2 0.7 fusion.4
  84.0 0.0 copy-done.3
  84.0 1.2 %fusion.1 = f32[8,3,544]{2,0,1:T(8,128)} fusion(f32[8,3,289]{2,0,1:T(8,128)S(1)} %fusion.4, f32[544,289]{0,1:T(8,128)S(1)} %copy-done), kind=kOutput, calls=%fused_computation.5 | convolution fusion | flops 45278208 | bytes 708832 | tf_op jit(solution)/shard_map/ckm,pm->ckp/dot_general | solution.py:133
  (11 shorter events, 0.2 us)
Async XLA Ops:
  0.6 2.7 %copy-start = (f32[544,289]{0,1:T(8,128)S(1)}, f32[544,289]{0,1:T(8,128)}, u32[]{:S(2)}) copy-start(f32[544,289]{0,1:T(8,128)} %param.8) | copy-start | bytes 1886596
  0.6 0.8 copy-start.4
  3.9 0.8 copy-start.2
  4.9 0.7 copy-start.6
  22.4 4.8 %copy-start.5 = (s32[64,4]{0,1:T(4,128)S(1)}, s32[64,4]{0,1:T(4,128)}, u32[]{:S(2)}) copy-start(s32[64,4]{0,1:T(4,128)} %param.11) | copy-start | bytes 3076
  22.4 8.8 %collective-permute-start = (f32[1,64,6,128]{3,2,1,0:T(8,128)S(1)}, f32[1,64,6,128]{3,2,1,0:T(8,128)S(1)}, u32[]{:S(2)}, u32[]{:S(2)}) collective-permute-start(f32[1,64,6,128]{3,2,1,0:T(8,128)S(1)} %broadcast_in_dim_reshape.3), channel_id=1, source_target_pairs={{0,16},{1,17},{2,18},{3,19},{4,20},{5,21},{6,22},{7,23},{8,24},{9,... | collective-permute-start | bytes 589832 | tf_op jit(solution)/shard_map/ppermute | solution.py:28
  25.9 9.6 %collective-permute-start.1 = (f32[1,64,6,128]{3,2,1,0:T(8,128)S(1)}, f32[1,64,6,128]{3,2,1,0:T(8,128)S(1)}, u32[]{:S(2)}, u32[]{:S(2)}) collective-permute-start(f32[1,64,6,128]{3,2,1,0:T(8,128)S(1)} %broadcast_in_dim_reshape.3), channel_id=1, source_target_pairs={{16,0},{17,1},{18,2},{19,3},{20,4},{21,5},{22,6},{23,7},{24,8},{25... | collective-permute-start | bytes 589832 | tf_op jit(solution)/shard_map/ppermute | solution.py:31
  36.4 46.8 %copy-start.1 = (f32[289,544]{1,0:T(8,128)S(1)}, f32[289,544]{1,0:T(8,128)}, u32[]{:S(2)}) copy-start(f32[289,544]{1,0:T(8,128)} %param.7) | copy-start | bytes 1886596
  83.2 0.8 copy-start.3

commit v2 on v1

--- a/solution.py
+++ b/solution.py
@@ -1,3 +1,4 @@
+import functools
 import math
 
 import jax
@@ -11,6 +12,7 @@
 LEAF = 128
 KNEAR = 4
 C_DEV = 8
+ROWS = 16
 BLK_DEV = 34
 
 
@@ -18,19 +20,6 @@
 KERNEL = 1.0 / (8.0 * math.pi)
 TIME_STEP = 0.02
 PRECISE = lax.Precision.HIGHEST
-
-
-def with_halo(block, sides, width):
-    for axis, dim in sides:
-        count = lax.axis_size(axis)
-        forward = [(i, i + 1) for i in range(count - 1)]
-        backward = [(target, source) for source, target in forward]
-        low = lax.ppermute(
-            lax.slice_in_dim(block, block.shape[dim] - width, None, axis=dim), axis, forward
-        )
-        high = lax.ppermute(lax.slice_in_dim(block, 0, width, axis=dim), axis, backward)
-        block = jnp.concatenate([low, block, high], axis=dim)
-    return block
 
 
 def split3(value):
@@ -46,7 +35,7 @@
     return first, (value - first.astype(jnp.float32)).astype(jnp.bfloat16)
 
 
-def near_kernel(lists_ref, near_ref, flows_ref, table_ref):
+def near_kernel(lists_ref, near_ref, flows_ref, table_ref, dist0_ref, dist1_ref, value0_ref, value1_ref):
     total = near_ref.shape[0]
     slot_count = flows_ref.shape[0]
     zeros4 = jnp.zeros((4, LEAF), jnp.float32)
@@ -74,35 +63,63 @@
     lax.fori_loop(0, total, prepare, 0, unroll=4)
     own = slot_count
 
-    def one_slot(slot, carry):
+    def distances(slot, out_ref):
         x = near_ref[own + slot][0:3]
         x_sq = jnp.sum(x * x, axis=0, keepdims=True)
         base = jnp.concatenate([x, ones, x_sq, jnp.zeros((3, LEAF), jnp.float32)], axis=0)
         t1, t2, t3 = [piece.astype(jnp.float32) for piece in split3(base)]
         target = jnp.concatenate([t1, t1, t1, t2, t2, t3], axis=0).T.astype(jnp.bfloat16)
-        total_c = None
         for entry in range(KNEAR):
             source = lists_ref[slot * KNEAR + entry]
-            rows = table_ref[source]
-            both = jnp.dot(target, rows[0:48], preferred_element_type=jnp.float32)
-            rr, projected = both[:, 0:LEAF], both[:, LEAF:]
-            inv = lax.rsqrt(rr)
-            inv3 = inv * inv * inv
-            a1, a2 = split2(inv + SOFTENING * inv3)
-            b1, b2 = split2(projected * inv3)
-            w_f, w_y = rows[48:64, 0:LEAF], rows[48:64, LEAF:]
-            values = jnp.concatenate([a1, a2, b1, b2], axis=1)
-            weights = jnp.concatenate([w_f, w_f, w_y, w_y], axis=1)
-            part = lax.dot_general(
-                values, weights, (((1,), (1,)), ((), ())), preferred_element_type=jnp.float32
+            out_ref[entry] = jnp.dot(
+                target, table_ref[source, 0:48], preferred_element_type=jnp.float32
             )
-            total_c = part if total_c is None else total_c + part
+
+    def kernels(in_ref, out_ref):
+        for entry in range(KNEAR):
+            for row in range(0, LEAF, ROWS):
+                rr = in_ref[entry, row : row + ROWS, 0:LEAF]
+                projected = in_ref[entry, row : row + ROWS, LEAF:]
+                inv = lax.rsqrt(rr)
+                inv3 = inv * inv * inv
+                parts = split2(inv + SOFTENING * inv3) + split2(projected * inv3)
+                for piece in range(4):
+                    start = (entry * 4 + piece) * LEAF
+                    out_ref[row : row + ROWS, start : start + LEAF] = parts[piece]
+
+    def sums(slot, in_ref):
+        weights = []
+        for entry in range(KNEAR):
+            source = lists_ref[slot * KNEAR + entry]
+            w_f = table_ref[source, 48:64, 0:LEAF]
+            w_y = table_ref[source, 48:64, LEAF:]
+            weights += [w_f, w_f, w_y, w_y]
+        total_c = lax.dot_general(
+            in_ref[...],
+            jnp.concatenate(weights, axis=1),
+            (((1,), (1,)), ((), ())),
+            preferred_element_type=jnp.float32,
+        )
         turned = total_c.T
         turned = turned[0:8] + turned[8:16]
+        x = near_ref[own + slot][0:3]
         flows_ref[slot] = turned[0:3] + x * turned[3:4]
-        return carry
-
-    lax.fori_loop(0, slot_count, one_slot, 0, unroll=2)
+
+    dist = (dist0_ref, dist1_ref)
+    value = (value0_ref, value1_ref)
+    distances(0, dist0_ref)
+    value1_ref[...] = jnp.zeros_like(value1_ref)
+
+    def pair(step, carry):
+        for parity in range(2):
+            slot = 2 * step + parity
+            distances(jnp.minimum(slot + 1, slot_count - 1), dist[1 - parity])
+            kernels(dist[parity], value[parity])
+            sums(jnp.maximum(slot - 1, 0), value[1 - parity])
+        return carry
+
+    lax.fori_loop(0, slot_count // 2, pair, 0)
+    sums(slot_count - 1, value1_ref)
 
 
 def near_sum(near_data, lists):
@@ -116,8 +133,166 @@
             pl.BlockSpec(memory_space=pltpu.VMEM),
         ],
         out_specs=pl.BlockSpec(memory_space=pltpu.VMEM),
-        scratch_shapes=[pltpu.VMEM((total, 64, 2 * LEAF), jnp.bfloat16)],
+        scratch_shapes=[
+            pltpu.VMEM((total, 64, 2 * LEAF), jnp.bfloat16),
+            pltpu.VMEM((KNEAR, LEAF, 2 * LEAF), jnp.float32),
+            pltpu.VMEM((KNEAR, LEAF, 2 * LEAF), jnp.float32),
+            pltpu.VMEM((LEAF, 4 * KNEAR * LEAF), jnp.bfloat16),
+            pltpu.VMEM((LEAF, 4 * KNEAR * LEAF), jnp.bfloat16),
+        ],
     )(lists.reshape(-1), near_data)
+
+
+MESH = pl.DeviceIdType.MESH
+
+
+def beside(group, groups, action):
+    pl.when(group + 1 < groups)(functools.partial(action, 0, group + 1))
+    pl.when(group > 0)(functools.partial(action, 1, group - 1))
+
+
+def greet(count, me, groups=None, group=None):
+    barrier = pltpu.get_barrier_semaphore()
+
+    def signal(step, carry):
+        pl.semaphore_signal(
+            barrier, inc=1, device_id={"dev": lax.rem(me + step, count)}, device_id_type=MESH
+        )
+        return carry
+
+    lax.fori_loop(1, count, signal, 0)
+    if groups is not None:
+
+        def signal_beside(way, other):
+            pl.semaphore_signal(barrier, inc=1, device_id={"group": other}, device_id_type=MESH)
+
+        beside(group, groups, signal_beside)
+        sides = jnp.minimum(group, 1) + jnp.minimum(groups - 1 - group, 1)
+        pl.semaphore_wait(barrier, count - 1 + sides)
+    else:
+        pl.semaphore_wait(barrier, count - 1)
+
+
+def forward_kernel(packed_ref, near_ref, own_sem, send_sem, recv_sem, side_send, side_recv):
+    count, groups = lax.axis_size("dev"), lax.axis_size("group")
+    me, group = lax.axis_index("dev"), lax.axis_index("group")
+    greet(count, me, groups, group)
+    own = pltpu.make_async_copy(packed_ref.at[me], near_ref.at[1, me], own_sem)
+    own.start()
+
+    def across(step):
+        peer = lax.rem(me + step, count)
+        return pltpu.make_async_remote_copy(
+            src_ref=packed_ref.at[peer],
+            dst_ref=near_ref.at[1, me],
+            send_sem=send_sem.at[step],
+            recv_sem=recv_sem.at[step],
+            device_id={"dev": peer},
+            device_id_type=MESH,
+        )
+
+    def along(step, way, other):
+        chunk = lax.rem(me - step + count, count)
+        return pltpu.make_async_remote_copy(
+            src_ref=near_ref.at[1, chunk],
+            dst_ref=near_ref.at[2 * way, chunk],
+            send_sem=side_send.at[way, step],
+            recv_sem=side_recv.at[way, step],
+            device_id={"group": other},
+            device_id_type=MESH,
+        )
+
+    def start(step, carry):
+        across(step).start()
+        return carry
+
+    lax.fori_loop(1, count, start, 0)
+
+    def clear(side):
+        near_ref[side] = jnp.zeros_like(near_ref[side])
+
+    pl.when(group == 0)(lambda: clear(0))
+    pl.when(group == groups - 1)(lambda: clear(2))
+    own.wait()
+    beside(group, groups, lambda way, other: along(0, way, other).start())
+
+    def relay(step, carry):
+        across(step).wait_recv()
+        beside(group, groups, lambda way, other: along(step, way, other).start())
+        return carry
+
+    lax.fori_loop(1, count, relay, 0)
+
+    def finish(step, carry):
+        pl.when(group + 1 < groups)(lambda: along(step, 0, group + 1).wait_send())
+        pl.when(group > 0)(lambda: along(step, 1, group - 1).wait_send())
+        pl.when(group > 0)(lambda: along(step, 0, group - 1).wait_recv())
+        pl.when(group + 1 < groups)(lambda: along(step, 1, group + 1).wait_recv())
+        return carry
+
+    lax.fori_loop(0, count, finish, 0)
+
+    def sent(step, carry):
+        across(step).wait_send()
+        return carry
+
+    lax.fori_loop(1, count, sent, 0)
+
+
+def forward(packed):
+    count = packed.shape[0]
+    sem = pltpu.SemaphoreType.DMA
+    return pl.pallas_call(
+        forward_kernel,
+        out_shape=jax.ShapeDtypeStruct((3,) + packed.shape, packed.dtype),
+        in_specs=[pl.BlockSpec(memory_space=pltpu.VMEM)],
+        out_specs=pl.BlockSpec(memory_space=pltpu.VMEM),
+        scratch_shapes=[sem, sem((count,)), sem((count,)), sem((2, count)), sem((2, count))],
+        compiler_params=pltpu.CompilerParams(collective_id=0, has_side_effects=True),
+    )(packed)
+
+
+def back_kernel(flows_ref, back_ref, own_sem, send_sem, recv_sem):
+    count, me = lax.axis_size("dev"), lax.axis_index("dev")
+    greet(count, me)
+    own = pltpu.make_async_copy(flows_ref.at[me], back_ref.at[me], own_sem)
+    own.start()
+
+    def across(step):
+        peer = lax.rem(me + step, count)
+        return pltpu.make_async_remote_copy(
+            src_ref=flows_ref.at[peer],
+            dst_ref=back_ref.at[me],
+            send_sem=send_sem.at[step],
+            recv_sem=recv_sem.at[step],
+            device_id={"dev": peer},
+            device_id_type=MESH,
+        )
+
+    def start(step, carry):
+        across(step).start()
+        return carry
+
+    def finish(step, carry):
+        across(step).wait()
+        return carry
+
+    lax.fori_loop(1, count, start, 0)
+    own.wait()
+    lax.fori_loop(1, count, finish, 0)
+
+
+def back(flows):
+    count = flows.shape[0]
+    sem = pltpu.SemaphoreType.DMA
+    return pl.pallas_call(
+        back_kernel,
+        out_shape=jax.ShapeDtypeStruct(flows.shape, flows.dtype),
+        in_specs=[pl.BlockSpec(memory_space=pltpu.VMEM)],
+        out_specs=pl.BlockSpec(memory_space=pltpu.VMEM),
+        scratch_shapes=[sem, sem((count,)), sem((count,))],
+        compiler_params=pltpu.CompilerParams(collective_id=1, has_side_effects=True),
+    )(flows)
 
 
 def to_blocks(values):
@@ -152,18 +327,10 @@
     payload = jnp.concatenate([to_blocks(shape_field), to_blocks(forces)], axis=1).reshape(
         BLK_DEV, 6 * LEAF
     )
-    packed = jnp.dot(onehot.T, payload, precision=PRECISE).reshape(dev_count, capacity, 6 * LEAF)
-    arrived = lax.all_to_all(packed, "dev", split_axis=0, concat_axis=0, tiled=True).reshape(
-        slot_count, 6, LEAF
-    )
-    near_data = with_halo(arrived[None], (("group", 0),), 1)
-    near_data = near_data.reshape(3 * slot_count, 6, LEAF)
-
-    flows = near_sum(near_data, ulist)
-    flows = flows.reshape(dev_count, capacity, 3 * LEAF)
-    returned = lax.all_to_all(flows, "dev", split_axis=0, concat_axis=0, tiled=True).reshape(
-        slot_count, 3 * LEAF
-    )
+    packed = jnp.dot(onehot.T, payload, precision=PRECISE).reshape(dev_count, capacity, 6, LEAF)
+    near_data = forward(packed).reshape(3 * slot_count, 6, LEAF)
+    flows = near_sum(near_data, ulist).reshape(dev_count, capacity, 3, LEAF)
+    returned = back(flows).reshape(slot_count, 3 * LEAF)
     velocity = from_blocks(jnp.dot(onehot, returned, precision=PRECISE).reshape(BLK_DEV, 3, LEAF))
     shape_field = filtered(shape_field + TIME_STEP * velocity, analysis, synthesis)
     return (shape_field, velocity)

time: 85.5 us -> 63.8 us (0.75)
  blocking collectives: 26.4 us -> 0 us
  Pallas kernels: 35.2 us -> 53.4 us
  waiting for transfers between devices: 7.48 us -> 0 us
  starting transfers between devices: 4.7 us -> 0 us
  local copies, waits for them, and re-layouts: 4.46 us -> 3.31 us
  other arithmetic: 1.18 us -> 0.22 us
  matrix products: 4.83 us -> 5.77 us
    all_to_all x2 -> x0, blocking collectives: 26.4 us -> none  [the longest x1 16.2 us: shards(): lax.all_to_all(packed, 'dev', split_axis=0, concat_axis=0, tiled=True)]
    pallas_call x0 -> x2, Pallas kernels: none -> 26.3 us  [the longest x1 17.7 us: forward(): pl.pallas_call(forward_kernel, out_shape=jax.ShapeDtypeStruct((3,) + pack...]
    pallas_call x1, Pallas kernels: 35.2 us -> 27.1 us  [near_sum(): pl.pallas_call(near_kernel, out_shape=jax.ShapeDtypeStruct((slot_count, 3...]
    ppermute x2 -> x0, waiting for transfers between devices: 7.48 us -> none  [the longest x1 4.13 us: with_halo(): lax.ppermute(lax.slice_in_dim(block, 0, width, axis=dim), axis, backward)]
    ppermute x2 -> x0, starting transfers between devices: 4.7 us -> none  [the longest x1 3.41 us: with_halo(): lax.ppermute(lax.slice_in_dim(block, block.shape[dim] - width, None, axis...]
    reshape x3 -> x0, local copies, waits for them, and re-layouts: 1.03 us -> none  [the longest x1 0.97 us: shards(): flows = flows.reshape(dev_count, capacity, 3 * LEAF)]
    concatenate x1 -> x0, other arithmetic: 0.95 us -> none  [with_halo(): block = jnp.concatenate([low, block, high], axis=dim)]
    dot_general x1, matrix products: 0.22 us -> 1.13 us  [shards(): jnp.dot(onehot, returned, precision=PRECISE).reshape(BLK_DEV, 3, LEAF)]
  transfers between devices with their start and end apart: 2 -> 0, of which waited for: 2 -> 0; matrix products, arithmetic and copies ran while one was open for 1% -> 0% of each run, Pallas kernels for 0% -> 0%
where the time goes in v2:
time: 63.8 us; the launch traced here: 63.5 us
  Pallas kernels  53.4 us (84%)
  matrix products  5.77 us (9%)
  local copies, waits for them, and re-layouts  3.31 us (5%)
  between operations  0.82 us (1%)
    pallas_call x1, Pallas kernels, near_sum(): pl.pallas_call(near_kernel, out_shape=jax.ShapeDtypeStruct((slot_count, 3...  27.1 us
    pallas_call x1, Pallas kernels, forward(): pl.pallas_call(forward_kernel, out_shape=jax.ShapeDtypeStruct((3,) + pack...  17.7 us
    pallas_call x1, Pallas kernels, back(): pl.pallas_call(back_kernel, out_shape=jax.ShapeDtypeStruct(flows.shape, f...  8.51 us
    dot_general x1, matrix products, shards(): coeffs = jnp.einsum('ckp,mp->ckm', shape_field, analysis, precision=PRECISE)  1.94 us
    unnamed x15, local copies, waits for them, and re-layouts  1.54 us

profile of v2, /device:TPU:0, one launch (start us, length us, event | category | flops | bytes accessed | tf_op | source)
XLA Modules:
  0.0 63.5 jit_solution(8260146789703304085)
XLA Ops:
  0.6 0.0 copy-start
  0.6 1.9 %convolution_multiply_fusion = f32[8,3,289]{2,0,1:T(8,128)S(1)} fusion(f32[8,3,544]{2,0,1:T(8,128)} %param.6, f32[289,544]{1,0:T(8,128)} %param.7, f32[289]{0:T(512)} %param.9), kind=kOutput, calls=%fused_computation.3 | convolution fusion | flops 45285144 | bytes 709988 | tf_op jit(solution)/shard_map/ckp,mp->ckm/dot_general | solution.py:325
  2.6 0.0 copy-done
  2.6 0.5 fusion
  3.1 0.0 copy-start.2
  3.1 0.1 reshape.55
  3.2 0.7 %copy-done.2 = f32[8,3,544]{2,0,1:T(8,128)S(1)} copy-done((f32[8,3,544]{2,0,1:T(8,128)S(1)}, f32[8,3,544]{2,0,1:T(8,128)}, u32[]{:S(2)}) %copy-start.2) | copy-done | bytes 52248
  4.0 0.1 reshape.54
  4.2 0.0 copy-start.5
  4.2 0.6 %copy-done.5 = s32[34,1]{0,1:T(1,128)S(1)} copy-done((s32[34,1]{0,1:T(1,128)S(1)}, s32[34,1]{0,1:T(1,128)}, u32[]{:S(2)}) %copy-start.5) | copy-done | bytes 160
  4.9 0.2 select_reduce_fusion
  5.1 0.3 fusion.7
  5.4 0.8 %copy.19.packed_ref = f32[16,4,6,128]{3,2,1,0:T(8,128)} copy(f32[16,4,6,128]{3,0,2,1:T(8,128)S(1)} %fusion.7) | data formatting | bytes 393216 | tf_op jit(solution)/shard_map/dot_general | solution.py:330
  6.1 0.0 copy-start.4
  6.2 17.7 %shard_map.77 = f32[3,16,4,6,128]{4,3,2,1,0:T(8,128)} custom-call(f32[16,4,6,128]{3,2,1,0:T(8,128)} %copy.19.packed_ref), custom_call_target="tpu_custom_call" | custom-call | tf_op jit(solution)/shard_map/pallas_call | solution.py:245
  23.9 0.0 copy-done.4
  23.9 0.1 copy.15
  24.0 0.0 copy-start.1
  24.0 0.7 %reshape.53.lists_ref = s32[256]{0:T(256)} reshape(s32[64,4]{1,0:T(8,128)S(1)} %copy.15) | data formatting | bytes 2048 | tf_op jit(solution)/shard_map/reshape | solution.py:143
  24.7 27.1 %shard_map.78 = f32[64,3,128]{2,1,0:T(4,128)} custom-call(s32[256]{0:T(256)} %reshape.53.lists_ref, f32[192,6,128]{2,1,0:T(8,128)} %bitcast.64), custom_call_target="tpu_custom_call" | custom-call | tf_op jit(solution)/shard_map/pallas_call | solution.py:128
  51.8 8.5 %shard_map.79 = f32[16,4,3,128]{3,2,1,0:T(4,128)} custom-call(f32[16,4,3,128]{3,2,1,0:T(4,128)} %bitcast.67), custom_call_target="tpu_custom_call" | custom-call | tf_op jit(solution)/shard_map/pallas_call | solution.py:288
  60.3 1.1 %convolution_bitcast_fusion = f32[3,34,128]{2,1,0:T(8,128)S(1)} fusion(s32[34]{0:T(128)S(1)} %fusion.23, f32[8,8,3,128]{3,2,1,0:T(4,128)} %bitcast.69), kind=kOutput, calls=%fused_computation | convolution fusion | flops 10029184 | bytes 150664 | tf_op jit(solution)/shard_map/dot_general | solution.py:334
  61.5 0.1 reshape.60
  61.6 0.0 copy-start.3
  61.6 0.0 copy-done.1
  61.6 0.7 %fusion.4 = f32[8,3,289]{2,0,1:T(8,128)S(1)} fusion(f32[289,544]{1,0:T(8,128)S(1)} %copy-done.1, f32[8,3,544]{2,0,1:T(8,128)S(1)} %copy-done.2, f32[8,3,544]{2,0,1:T(8,128)S(1)} %bitcast.70), kind=kOutput, calls=%fused_computation.7 | convolution fusion | flops 45304320 | bytes 761056 | tf_op jit(solution)/shard_map/ckp,mp->ckm/dot_general | solution.py:307
  62.3 0.0 copy-done.3
  62.4 1.2 %fusion.1 = f32[8,3,544]{2,0,1:T(8,128)} fusion(f32[8,3,289]{2,0,1:T(8,128)S(1)} %fusion.4, f32[544,289]{0,1:T(8,128)S(1)} %copy-done), kind=kOutput, calls=%fused_computation.4 | convolution fusion | flops 45278208 | bytes 708832 | tf_op jit(solution)/shard_map/ckm,pm->ckp/dot_general | solution.py:308
  (7 shorter events, 0.1 us)
Async XLA Ops:
  0.6 2.0 %copy-start = (f32[544,289]{0,1:T(8,128)S(1)}, f32[544,289]{0,1:T(8,128)}, u32[]{:S(2)}) copy-start(f32[544,289]{0,1:T(8,128)} %param.8) | copy-start | bytes 1886596
  3.1 0.8 %copy-start.2 = (f32[8,3,544]{2,0,1:T(8,128)S(1)}, f32[8,3,544]{2,0,1:T(8,128)}, u32[]{:S(2)}) copy-start(f32[8,3,544]{2,0,1:T(8,128)} %param.6) | copy-start | bytes 156676
  4.2 0.7 %copy-start.5 = (s32[34,1]{0,1:T(1,128)S(1)}, s32[34,1]{0,1:T(1,128)}, u32[]{:S(2)}) copy-start(s32[34,1]{0,1:T(1,128)} %param.10) | copy-start | bytes 412
  6.1 17.8 %copy-start.4 = (s32[64,4]{0,1:T(4,128)S(1)}, s32[64,4]{0,1:T(4,128)}, u32[]{:S(2)}) copy-start(s32[64,4]{0,1:T(4,128)} %param.11) | copy-start | bytes 3076
  24.0 37.6 %copy-start.1 = (f32[289,544]{1,0:T(8,128)S(1)}, f32[289,544]{1,0:T(8,128)}, u32[]{:S(2)}) copy-start(f32[289,544]{1,0:T(8,128)} %param.7) | copy-start | bytes 1886596
  61.6 0.8 %copy-start.3 = (f32[3,8,544]{2,1,0:T(8,128)}, f32[3,8,544]{2,1,0:T(8,128)S(1)}, u32[]{:S(2)}) copy-start(f32[3,8,544]{2,1,0:T(8,128)S(1)} %reshape.60) | copy-start | bytes 156676

commit v3 on v2

--- a/solution.py
+++ b/solution.py
@@ -13,6 +13,7 @@
 KNEAR = 4
 C_DEV = 8
 ROWS = 16
+WIDTH = 4
 BLK_DEV = 34
 
 
@@ -35,18 +36,23 @@
     return first, (value - first.astype(jnp.float32)).astype(jnp.bfloat16)
 
 
-def near_kernel(lists_ref, near_ref, flows_ref, table_ref, dist0_ref, dist1_ref, value0_ref, value1_ref):
-    total = near_ref.shape[0]
+def near_kernel(
+    lists_ref, near_ref, flows_ref, table_ref, target_ref, total_ref,
+    dist0_ref, dist1_ref, value0_ref, value1_ref, item_slot, item_source,
+):
     slot_count = flows_ref.shape[0]
     zeros4 = jnp.zeros((4, LEAF), jnp.float32)
     ones = jnp.ones((1, LEAF), jnp.float32)
-
-    def prepare(slot, carry):
+    low, high = lists_ref[slot_count * KNEAR], lists_ref[slot_count * KNEAR + 1]
+
+    def prepare(slot):
         data = near_ref[slot]
         y, f = data[0:3], data[3:6]
-        y_sq = jnp.sum(y * y, axis=0, keepdims=True) + SOFTENING
+        y_sq = jnp.sum(y * y, axis=0, keepdims=True)
         yf = -jnp.sum(y * f, axis=0, keepdims=True)
-        dist = jnp.concatenate([-2.0 * y, y_sq, ones, jnp.zeros((3, LEAF), jnp.float32)], axis=0)
+        dist = jnp.concatenate(
+            [-2.0 * y, y_sq + SOFTENING, ones, jnp.zeros((3, LEAF), jnp.float32)], axis=0
+        )
         proj = jnp.concatenate([f, yf, zeros4], axis=0)
         d1, d2, d3 = [piece.astype(jnp.float32) for piece in split3(dist)]
         p1, p2, p3 = [piece.astype(jnp.float32) for piece in split3(proj)]
@@ -58,73 +64,103 @@
         right = jnp.concatenate([p1, p2, p3, p1, p2, p1, y1, y2], axis=0)
         table_ref[slot, :, 0:LEAF] = left.astype(jnp.bfloat16)
         table_ref[slot, :, LEAF:] = right.astype(jnp.bfloat16)
-        return carry
-
-    lax.fori_loop(0, total, prepare, 0, unroll=4)
-    own = slot_count
-
-    def distances(slot, out_ref):
-        x = near_ref[own + slot][0:3]
-        x_sq = jnp.sum(x * x, axis=0, keepdims=True)
+        return y, y_sq
+
+    def own_slot(slot, count):
+        x, x_sq = prepare(slot_count + slot)
         base = jnp.concatenate([x, ones, x_sq, jnp.zeros((3, LEAF), jnp.float32)], axis=0)
         t1, t2, t3 = [piece.astype(jnp.float32) for piece in split3(base)]
-        target = jnp.concatenate([t1, t1, t1, t2, t2, t3], axis=0).T.astype(jnp.bfloat16)
+        target = jnp.concatenate([t1, t1, t1, t2, t2, t3], axis=0)
+        target_ref[slot] = target.T.astype(jnp.bfloat16)
+        total_ref[slot] = jnp.zeros((8, LEAF), jnp.float32)
         for entry in range(KNEAR):
             source = lists_ref[slot * KNEAR + entry]
-            out_ref[entry] = jnp.dot(
-                target, table_ref[source, 0:48], preferred_element_type=jnp.float32
+            item_slot[count] = slot
+            item_source[count] = source
+            count = count + jnp.where((source >= low) & (source < high), 1, 0)
+        return count
+
+    def four(step, carry):
+        for place in range(4):
+            prepare(4 * step + place)
+        return carry
+
+    count = lax.fori_loop(0, slot_count, own_slot, 0, unroll=4)
+    lax.fori_loop(low // 4, slot_count // 4, four, 0)
+    lax.fori_loop(slot_count // 2, high // 4, four, 0)
+    target_ref[slot_count] = target_ref[0]
+    total_ref[slot_count] = jnp.zeros((8, LEAF), jnp.float32)
+    for extra in range(2 * WIDTH):
+        item_slot[count + extra] = slot_count
+        item_source[count + extra] = slot_count
+
+    def distances(group, out_ref):
+        for place in range(WIDTH):
+            item = group * WIDTH + place
+            out_ref[place] = jnp.dot(
+                target_ref[item_slot[item]],
+                table_ref[item_source[item], 0:48],
+                preferred_element_type=jnp.float32,
             )
 
     def kernels(in_ref, out_ref):
-        for entry in range(KNEAR):
+        for place in range(WIDTH):
             for row in range(0, LEAF, ROWS):
-                rr = in_ref[entry, row : row + ROWS, 0:LEAF]
-                projected = in_ref[entry, row : row + ROWS, LEAF:]
+                rr = in_ref[place, row : row + ROWS, 0:LEAF]
+                projected = in_ref[place, row : row + ROWS, LEAF:]
                 inv = lax.rsqrt(rr)
                 inv3 = inv * inv * inv
                 parts = split2(inv + SOFTENING * inv3) + split2(projected * inv3)
                 for piece in range(4):
-                    start = (entry * 4 + piece) * LEAF
-                    out_ref[row : row + ROWS, start : start + LEAF] = parts[piece]
-
-    def sums(slot, in_ref):
-        weights = []
-        for entry in range(KNEAR):
-            source = lists_ref[slot * KNEAR + entry]
+                    start = piece * LEAF
+                    out_ref[place, row : row + ROWS, start : start + LEAF] = parts[piece]
+
+    def sums(group, in_ref):
+        for place in range(WIDTH):
+            item = group * WIDTH + place
+            source = item_source[item]
             w_f = table_ref[source, 48:64, 0:LEAF]
             w_y = table_ref[source, 48:64, LEAF:]
-            weights += [w_f, w_f, w_y, w_y]
-        total_c = lax.dot_general(
-            in_ref[...],
-            jnp.concatenate(weights, axis=1),
-            (((1,), (1,)), ((), ())),
-            preferred_element_type=jnp.float32,
-        )
-        turned = total_c.T
-        turned = turned[0:8] + turned[8:16]
-        x = near_ref[own + slot][0:3]
-        flows_ref[slot] = turned[0:3] + x * turned[3:4]
+            part = lax.dot_general(
+                jnp.concatenate([w_f, w_f, w_y, w_y], axis=1),
+                in_ref[place],
+                (((1,), (1,)), ((), ())),
+                preferred_element_type=jnp.float32,
+            )
+            total_ref[item_slot[item]] += part[0:8] + part[8:16]
 
     dist = (dist0_ref, dist1_ref)
     value = (value0_ref, value1_ref)
     distances(0, dist0_ref)
     value1_ref[...] = jnp.zeros_like(value1_ref)
+    pairs = (count + 2 * WIDTH - 1) // (2 * WIDTH)
 
     def pair(step, carry):
         for parity in range(2):
-            slot = 2 * step + parity
-            distances(jnp.minimum(slot + 1, slot_count - 1), dist[1 - parity])
+            group = 2 * step + parity
+            distances(jnp.minimum(group + 1, 2 * pairs - 1), dist[1 - parity])
             kernels(dist[parity], value[parity])
-            sums(jnp.maximum(slot - 1, 0), value[1 - parity])
-        return carry
-
-    lax.fori_loop(0, slot_count // 2, pair, 0)
-    sums(slot_count - 1, value1_ref)
+            sums(jnp.maximum(group - 1, 0), value[1 - parity])
+        return carry
+
+    lax.fori_loop(0, pairs, pair, 0)
+    sums(2 * pairs - 1, value1_ref)
+
+    def finish(slot, carry):
+        turned = total_ref[slot]
+        flows_ref[slot] = turned[0:3] + near_ref[slot_count + slot][0:3] * turned[3:4]
+        return carry
+
+    lax.fori_loop(0, slot_count, finish, 0, unroll=8)
 
 
 def near_sum(near_data, lists):
     total = near_data.shape[0]
     slot_count = lists.shape[0]
+    group, groups = lax.axis_index("group"), lax.axis_size("group")
+    low = jnp.where(group == 0, slot_count, 0)
+    high = jnp.where(group == groups - 1, 2 * slot_count, 3 * slot_count)
+    items = slot_count * KNEAR + 4 * WIDTH
     return pl.pallas_call(
         near_kernel,
         out_shape=jax.ShapeDtypeStruct((slot_count, 3, LEAF), jnp.float32),
@@ -135,12 +171,16 @@
         out_specs=pl.BlockSpec(memory_space=pltpu.VMEM),
         scratch_shapes=[
             pltpu.VMEM((total, 64, 2 * LEAF), jnp.bfloat16),
-            pltpu.VMEM((KNEAR, LEAF, 2 * LEAF), jnp.float32),
-            pltpu.VMEM((KNEAR, LEAF, 2 * LEAF), jnp.float32),
-            pltpu.VMEM((LEAF, 4 * KNEAR * LEAF), jnp.bfloat16),
-            pltpu.VMEM((LEAF, 4 * KNEAR * LEAF), jnp.bfloat16),
+            pltpu.VMEM((slot_count + 1, LEAF, 48), jnp.bfloat16),
+            pltpu.VMEM((slot_count + 1, 8, LEAF), jnp.float32),
+            pltpu.VMEM((WIDTH, LEAF, 2 * LEAF), jnp.float32),
+            pltpu.VMEM((WIDTH, LEAF, 2 * LEAF), jnp.float32),
+            pltpu.VMEM((WIDTH, LEAF, 4 * LEAF), jnp.bfloat16),
+            pltpu.VMEM((WIDTH, LEAF, 4 * LEAF), jnp.bfloat16),
+            pltpu.SMEM((items,), jnp.int32),
+            pltpu.SMEM((items,), jnp.int32),
         ],
-    )(lists.reshape(-1), near_data)
+    )(jnp.concatenate([lists.reshape(-1), jnp.stack([low, high])]), near_data)
 
 
 MESH = pl.DeviceIdType.MESH

time: 63.8 us -> 56.5 us (0.89)
  Pallas kernels: 53.4 us -> 45.3 us
  other arithmetic: 0.22 us -> 0.88 us
    pallas_call x1, Pallas kernels: 27.1 us -> 18.6 us  [near_sum(): pl.pallas_call(near_kernel, out_shape=jax.ShapeDtypeStruct((slot_count, 3...]
    unnamed x15, local copies, waits for them, and re-layouts: 1.54 us -> 2.21 us
    concatenate x0 -> x1, other arithmetic: none -> 0.66 us  [near_sum(): jnp.concatenate([lists.reshape(-1), jnp.stack([low, high])])]
where the time goes in v3:
time: 56.5 us; the launch traced here: 56.2 us
  Pallas kernels  45.3 us (80%)
  matrix products  5.77 us (10%)
  local copies, waits for them, and re-layouts  3.41 us (6%)
  other arithmetic  0.88 us (2%)
  between operations  0.83 us (1%)
    pallas_call x1, Pallas kernels, near_sum(): pl.pallas_call(near_kernel, out_shape=jax.ShapeDtypeStruct((slot_count, 3...  18.6 us
    pallas_call x1, Pallas kernels, forward(): pl.pallas_call(forward_kernel, out_shape=jax.ShapeDtypeStruct((3,) + pack...  17.7 us
    pallas_call x1, Pallas kernels, back(): pl.pallas_call(back_kernel, out_shape=jax.ShapeDtypeStruct(flows.shape, f...  8.91 us
    unnamed x15, local copies, waits for them, and re-layouts  2.21 us
    dot_general x1, matrix products, shards(): coeffs = jnp.einsum('ckp,mp->ckm', shape_field, analysis, precision=PRECISE)  1.94 us
    dot_general x1, matrix products, filtered(): return jnp.einsum('ckm,pm->ckp', coeffs, synthesis, precision=PRECISE)  1.15 us

profile of v3, /device:TPU:0, one launch (start us, length us, event | category | flops | bytes accessed | tf_op | source)
XLA Modules:
  0.0 56.2 jit_solution(4434257110906377911)
XLA Ops:
  0.6 0.0 copy-start
  0.6 1.9 %convolution_multiply_fusion = f32[8,3,289]{2,0,1:T(8,128)S(1)} fusion(f32[8,3,544]{2,0,1:T(8,128)} %param.6, f32[289,544]{1,0:T(8,128)} %param.7, f32[289]{0:T(512)} %param.9), kind=kOutput, calls=%fused_computation.3 | convolution fusion | flops 45285144 | bytes 709988 | tf_op jit(solution)/shard_map/ckp,mp->ckm/dot_general | solution.py:365
  2.6 0.0 copy-done
  2.6 0.5 fusion
  3.1 0.0 copy-start.2
  3.1 0.1 reshape.55
  3.2 0.7 %copy-done.2 = f32[8,3,544]{2,0,1:T(8,128)S(1)} copy-done((f32[8,3,544]{2,0,1:T(8,128)S(1)}, f32[8,3,544]{2,0,1:T(8,128)}, u32[]{:S(2)}) %copy-start.2) | copy-done | bytes 52248
  4.0 0.1 reshape.54
  4.2 0.0 copy-start.5
  4.2 0.6 %copy-done.5 = s32[34,1]{0,1:T(1,128)S(1)} copy-done((s32[34,1]{0,1:T(1,128)S(1)}, s32[34,1]{0,1:T(1,128)}, u32[]{:S(2)}) %copy-start.5) | copy-done | bytes 160
  4.9 0.2 select_reduce_fusion
  5.1 0.3 fusion.7
  5.4 0.8 %copy.19.packed_ref = f32[16,4,6,128]{3,2,1,0:T(8,128)} copy(f32[16,4,6,128]{3,0,2,1:T(8,128)S(1)} %fusion.7) | data formatting | bytes 393216 | tf_op jit(solution)/shard_map/dot_general | solution.py:370
  6.1 17.7 %shard_map.77 = f32[3,16,4,6,128]{4,3,2,1,0:T(8,128)} custom-call(f32[16,4,6,128]{3,2,1,0:T(8,128)} %copy.19.packed_ref), custom_call_target="tpu_custom_call" | custom-call | tf_op jit(solution)/shard_map/pallas_call | solution.py:285
  23.9 0.0 copy-start.4
  23.9 0.7 %copy-done.4 = s32[64,4]{0,1:T(4,128)S(1)} copy-done((s32[64,4]{0,1:T(4,128)S(1)}, s32[64,4]{0,1:T(4,128)}, u32[]{:S(2)}) %copy-start.4) | copy-done | bytes 1048
  24.6 0.1 copy.15
  24.7 0.0 copy-start.1
  24.7 0.1 reshape.53
  24.8 0.7 %pad_add_fusion.lists_ref = s32[258]{0:T(512)} fusion(s32[1]{0:T(128)} %bitcast.5, s32[1]{0:T(128)} %bitcast.4, s32[256]{0:T(256)S(1)} %reshape.53), kind=kLoop, calls=%fused_computation.32 | loop fusion | flops 516 | bytes 2064 | tf_op jit(solution)/shard_map/concatenate | solution.py:183
  25.4 18.6 %shard_map.78 = f32[64,3,128]{2,1,0:T(4,128)} custom-call(s32[258]{0:T(512)} %pad_add_fusion.lists_ref, f32[192,6,128]{2,1,0:T(8,128)} %bitcast.66), custom_call_target="tpu_custom_call" | custom-call | tf_op jit(solution)/shard_map/pallas_call | solution.py:164
  44.1 8.9 %shard_map.79 = f32[16,4,3,128]{3,2,1,0:T(4,128)} custom-call(f32[16,4,3,128]{3,2,1,0:T(4,128)} %bitcast.69), custom_call_target="tpu_custom_call" | custom-call | tf_op jit(solution)/shard_map/pallas_call | solution.py:328
  53.0 1.1 %convolution_bitcast_fusion = f32[3,34,128]{2,1,0:T(8,128)S(1)} fusion(s32[34]{0:T(128)S(1)} %fusion.23, f32[8,8,3,128]{3,2,1,0:T(4,128)} %bitcast.71), kind=kOutput, calls=%fused_computation | convolution fusion | flops 10029184 | bytes 150664 | tf_op jit(solution)/shard_map/dot_general | solution.py:374
  54.1 0.1 reshape.60
  54.2 0.0 copy-start.3
  54.2 0.0 copy-done.1
  54.3 0.7 %fusion.4 = f32[8,3,289]{2,0,1:T(8,128)S(1)} fusion(f32[289,544]{1,0:T(8,128)S(1)} %copy-done.1, f32[8,3,544]{2,0,1:T(8,128)S(1)} %copy-done.2, f32[8,3,544]{2,0,1:T(8,128)S(1)} %bitcast.72), kind=kOutput, calls=%fused_computation.7 | convolution fusion | flops 45304320 | bytes 761056 | tf_op jit(solution)/shard_map/ckp,mp->ckm/dot_general | solution.py:347
  55.0 0.0 copy-done.3
  55.0 1.2 %fusion.1 = f32[8,3,544]{2,0,1:T(8,128)} fusion(f32[8,3,289]{2,0,1:T(8,128)S(1)} %fusion.4, f32[544,289]{0,1:T(8,128)S(1)} %copy-done), kind=kOutput, calls=%fused_computation.4 | convolution fusion | flops 45278208 | bytes 708832 | tf_op jit(solution)/shard_map/ckm,pm->ckp/dot_general | solution.py:348
  (7 shorter events, 0.1 us)
Async XLA Ops:
  0.6 2.0 %copy-start = (f32[544,289]{0,1:T(8,128)S(1)}, f32[544,289]{0,1:T(8,128)}, u32[]{:S(2)}) copy-start(f32[544,289]{0,1:T(8,128)} %param.8) | copy-start | bytes 1886596
  3.1 0.8 %copy-start.2 = (f32[8,3,544]{2,0,1:T(8,128)S(1)}, f32[8,3,544]{2,0,1:T(8,128)}, u32[]{:S(2)}) copy-start(f32[8,3,544]{2,0,1:T(8,128)} %param.6) | copy-start | bytes 156676
  4.2 0.7 %copy-start.5 = (s32[34,1]{0,1:T(1,128)S(1)}, s32[34,1]{0,1:T(1,128)}, u32[]{:S(2)}) copy-start(s32[34,1]{0,1:T(1,128)} %param.10) | copy-start | bytes 412
  23.9 0.7 %copy-start.4 = (s32[64,4]{0,1:T(4,128)S(1)}, s32[64,4]{0,1:T(4,128)}, u32[]{:S(2)}) copy-start(s32[64,4]{0,1:T(4,128)} %param.11) | copy-start | bytes 3076
  24.7 29.6 %copy-start.1 = (f32[289,544]{1,0:T(8,128)S(1)}, f32[289,544]{1,0:T(8,128)}, u32[]{:S(2)}) copy-start(f32[289,544]{1,0:T(8,128)} %param.7) | copy-start | bytes 1886596
  54.2 0.8 %copy-start.3 = (f32[3,8,544]{2,1,0:T(8,128)}, f32[3,8,544]{2,1,0:T(8,128)S(1)}, u32[]{:S(2)}) copy-start(f32[3,8,544]{2,1,0:T(8,128)S(1)} %reshape.60) | copy-start | bytes 156676
